TPU v7x, 512 devices: a whole 4x4x16 slice. The times are simulated.
512 devices in a mesh: dp: 64 (over x, z_lo, core), mp: 8 (over y, z_hi).
Axes of the slice: x: 4, y: 4, z: 16 (z_hi: 2, z_lo: 8; z = z_hi * 8 + z_lo), core: 2. Of those that a mesh axis runs over, the one named last changes fastest.
Arguments:
- master: float32 [8, 256, 512], P('mp', 'dp'), may hold values from -4 to 4
- moment: float32 [8, 256, 512], P('mp', 'dp'), may hold values from -0.06 to 0.06
- variance: float32 [8, 256, 512], P('mp', 'dp'), may hold values from 3e-06 to 3e-05
- flat_slot: int32 [256], replicated, may hold values from 0 to 255, each once
- feedback: bfloat16 [64, 2, 64, 8192], P('dp', None, 'mp'), may hold values from -0.029907227 to 0.029907227
- activations: bfloat16 [2, 8192, 8192], P(None, ('dp', 'mp')), may hold values from -24 to 24
- output_grads: bfloat16 [2, 8192, 8192], P(None, ('dp', 'mp')), may hold values from -24 to 24
Outputs:
- master_out: float32 [8, 256, 512], P('mp', 'dp')
- moment_out: float32 [8, 256, 512], P('mp', 'dp')
- feedback_out: bfloat16 [64, 2, 64, 8192], P('dp', None, 'mp')
Inputs may be any that keep to these rules, and one draw needn't show every extreme that they name: `flat_slot`: every position of the flat buffer holds exactly one of the 256 segments.
All inputs are finite; a program needn't handle non-finite values. Where the computation divides by a largest or mean magnitude, that divisor is 1e-20 or more.
Results may differ from a plain program's by a relative error of at most 0.0036.
The roundings to bfloat16 on the way count: a program that leaves them out, or rounds other values in their place, can miss the bound.
Values may be sent and summed in bfloat16 or wider, within the bound.
A program may use at most 64 MiB of HBM per device.

v0:
```python
import jax
import jax.numpy as jnp
from jax import lax
from jax.sharding import PartitionSpec as P

beta_one = 0.9
step_rate = 0.05
epsilon = 1e-08
down_scale = 28672.0 ** (-0.5)


def silu_slope(preact):
    sigmoid_value = jax.nn.sigmoid(preact)
    return sigmoid_value * (1.0 + preact * (1.0 - sigmoid_value))


def gradients(weights, inputs, cotangent, model_width):
    up_scale = model_width ** (-0.5)
    before = up_scale * jnp.dot(inputs, weights[0].T, preferred_element_type=jnp.float32)
    hidden = jax.nn.silu(before).astype(jnp.bfloat16)
    back_grad = down_scale * jnp.dot(cotangent, weights[1].T, preferred_element_type=jnp.float32)
    slope_grad = (back_grad * silu_slope(before)).astype(jnp.bfloat16)
    grad_up = up_scale * jnp.dot(slope_grad.T, inputs, preferred_element_type=jnp.float32)
    grad_down = down_scale * jnp.dot(hidden.T, cotangent, preferred_element_type=jnp.float32)
    return jnp.stack([grad_up, grad_down])


def per_device(master, moment, variance, flat_slot, feedback, activations, output_grads):
    owner_rows = master.shape[1]
    total_rows = flat_slot.shape[0]
    hidden_rows = feedback.shape[2]
    model_width = feedback.shape[3]
    workers = lax.axis_size("dp")
    tensor_shape = (2, hidden_rows, model_width)
    segment_shape = (total_rows, master.shape[2])
    inverse = (
        jnp.zeros((total_rows,), jnp.int32)
        .at[flat_slot]
        .set(jnp.arange(total_rows, dtype=jnp.int32))
    )
    working_flat = lax.all_gather(master[0].astype(jnp.bfloat16), "dp", axis=0, tiled=True)
    moment_flat, variance_flat = (
        lax.all_gather(moment[0], "dp", axis=0, tiled=True),
        lax.all_gather(variance[0], "dp", axis=0, tiled=True),
    )
    working = working_flat[flat_slot].reshape(tensor_shape)
    moment_t = moment_flat[flat_slot].reshape(tensor_shape)
    denominator = jnp.sqrt(variance_flat[flat_slot].reshape(tensor_shape)) + epsilon
    group_inputs, group_grads = (
        lax.all_gather(activations, "mp", axis=1, tiled=True),
        lax.all_gather(output_grads, "mp", axis=1, tiled=True),
    )
    step_one = gradients(working, group_inputs[0], group_grads[0], model_width)
    local_moment = beta_one * moment_t + (1.0 - beta_one) * step_one
    local_weights = (working.astype(jnp.float32) - step_rate * local_moment / denominator).astype(
        jnp.bfloat16
    )
    step_two = gradients(local_weights, group_inputs[1], group_grads[1], model_width)
    shifted = local_moment + feedback[0].astype(jnp.float32)
    magnitude = jnp.mean(jnp.abs(shifted), axis=-1, keepdims=True) + 1e-06
    packed = magnitude * jnp.tanh(shifted / magnitude)
    new_error = (shifted - packed).astype(jnp.bfloat16)
    first_row = lax.axis_index("dp") * owner_rows
    grad_flat = step_two.reshape(segment_shape)[inverse]
    moment_whole = lax.psum(packed, "dp")
    own_segments = lax.dynamic_slice_in_dim(inverse, first_row, owner_rows, 0)
    moment_own = moment_whole.reshape(segment_shape)[own_segments]
    grad_own = lax.psum_scatter(grad_flat, "dp", scatter_dimension=0, tiled=True)
    mean_moment = moment_own / workers
    mean_grad = grad_own / workers
    moment_new = beta_one * mean_moment + (1.0 - beta_one) * mean_grad
    owner_denominator = jnp.sqrt(variance[0]) + epsilon
    master_new = master[0] - step_rate * (mean_moment + moment_new) / owner_denominator
    return (master_new[None], moment_new[None], new_error[None])


def solution(mesh):
    in_specs = (
        P("mp", "dp", None),
        P("mp", "dp", None),
        P("mp", "dp", None),
        P(),
        P("dp", None, "mp", None),
        P(None, ("dp", "mp"), None),
        P(None, ("dp", "mp"), None),
    )
    out_specs = (P("mp", "dp", None), P("mp", "dp", None), P("dp", None, "mp", None))
    return jax.shard_map(
        per_device, mesh=mesh, in_specs=in_specs, out_specs=out_specs, check_vma=False
    )
```

profile of v0, /device:TPU:1, one launch (start us, length us, event | category | flops | bytes accessed | tf_op | source)
XLA Modules:
  0.0 1362.9 jit_solution(14703939547487024372)
XLA Ops:
  7.2 0.0 all-gather.8.cloned.1.call-start
  7.2 0.7 all-gather.8.cloned.1.call-update
  7.9 0.0 all-gather.6.cloned.1.call-start
  7.9 0.7 all-gather.6.cloned.1.call-update
  8.6 0.0 all-reduce.4.cloned.1.call-start
  8.7 0.7 copy.10
  9.4 181.0 %all-gather = f32[1,256,512]{2,0,1:T(1,128)S(1)} all-gather(f32[1,4,512]{2,0,1:T(1,128)S(1)} %copy.10), channel_id=2, replica_groups=mesh['dp'=64,'mp'=8] {'dp'}, dimensions={1}, use_global_device_ids=true | all-gather | bytes 532480 | tf_op jit(solution)/shard_map/all_gather | solution.py:43
  190.5 0.0 copy-start.2
  190.5 0.7 compare_select_fusion.1
  191.2 1.0 gather_fusion
  192.1 0.0 copy-start.3
  192.1 0.1 broadcast_multiply_fusion
  192.2 0.1 mul.139
  192.3 0.1 mul.173
  192.4 0.0 copy-done.2
  192.4 172.0 %all-gather.2 = bf16[64,4,512]{2,1,0:T(4,128)(2,1)S(1)} all-gather(bf16[1,4,512]{2,1,0:T(4,128)(2,1)S(1)} %fusion.24), channel_id=1, replica_groups=mesh['dp'=64,'mp'=8] {'dp'}, dimensions={0}, use_global_device_ids=true | all-gather | bytes 266240 | tf_op jit(solution)/shard_map/all_gather | solution.py:41
  364.4 0.1 reshape.144
  364.5 1.2 gather_fusion.1
  365.6 0.1 reshape.83
  365.8 0.0 copy-done.3
  365.8 114.9 %all-gather.1 = f32[1,256,512]{2,0,1:T(1,128)S(1)} all-gather(f32[1,4,512]{2,0,1:T(1,128)S(1)} %copy.11), channel_id=3, replica_groups=mesh['dp'=64,'mp'=8] {'dp'}, dimensions={1}, use_global_device_ids=true | all-gather | bytes 532480 | tf_op jit(solution)/shard_map/all_gather | solution.py:44
  480.7 1.0 gather_fusion.3
  481.7 0.1 sqrt_add_fusion
  481.8 0.1 add.91
  481.9 0.1 squeeze.40
  482.0 0.1 squeeze.38
  482.1 1.4 scatter_custom_fusion
  483.5 1.3 dynamic-slice
  485.4 0.1 compare_select_fusion.2
  485.5 0.0 copy-start
  485.5 0.0 all-gather.8.cloned.1.call-done
  485.6 2.3 fusion.12
  487.8 0.0 all-gather.6.cloned.1.call-done
  487.8 2.0 convolution_multiply_fusion.2
  489.8 3.8 convolution_multiply_fusion.3
  493.6 0.0 copy-done
  493.6 0.2 abs_reduce_fusion
  493.8 0.9 subtract_convert_fusion.1
  494.8 0.0 copy-start.1
  494.8 0.9 reshape.80
  495.7 2.3 fusion.7
  498.0 2.0 fusion
  500.0 0.0 copy-done.1
  500.0 3.8 fusion.1
  503.8 0.1 reshape.81
  503.9 1.8 gather_fusion.4
  505.8 0.0 all-reduce.4.cloned.1.call-update
  505.8 0.9 subtract_convert_fusion
  506.6 846.8 %all-reduce.4.cloned.1.call-done = (f32[256,512]{1,0:T(8,128)}, f32[256,512]{1,0:T(8,128)}) async-done(((f32[256,512]{1,0:T(8,128)}, f32[256,512]{1,0:T(8,128)}), (f32[256,512]{1,0:T(8,128)}, f32[256,512]{1,0:T(8,128)})) %all-reduce.4.cloned.1.call-update) | async-done | bytes 1048592 | tf_op jit(solution)/shard_map/psum | solution.py:65
  1353.5 1.6 gather_fusion.2
  1355.1 1.3 fusion.33
  (12 shorter events, 0.2 us)
Async XLA Ops:
  7.2 478.4 %all-gather.8.cloned.1.call-start = ((), (), s32[]{:S(2)}) async-start(), calls=%async_computation.1 | async-start | bytes 4718592 | tf_op jit(solution)/shard_map/all_gather | solution.py:50
  7.9 480.0 %all-gather.6.cloned.1.call-start = ((), (), s32[]{:S(2)}) async-start(), calls=%async_computation | async-start | bytes 4718592 | tf_op jit(solution)/shard_map/all_gather | solution.py:51
  8.6 1344.8 %all-reduce.4.cloned.1.call-start = ((), (), s32[]{:S(2)}) async-start(), calls=%async_computation.2 | async-start | bytes 2097152 | tf_op jit(solution)/shard_map/psum | solution.py:65
  190.5 2.0 copy-start.2
  192.1 173.6 %copy-start.3 = (f32[1,4,512]{2,1,0:T(4,128)S(1)}, f32[1,4,512]{2,1,0:T(4,128)}, u32[]{:S(2)}) copy-start(f32[1,4,512]{2,1,0:T(4,128)} %param.9) | copy-start | bytes 24580
  485.5 8.1 copy-start
  494.8 5.2 copy-start.1
Sparse Core Ops, SparseCore 0:
  11.2 185.7 all-gather.7
  200.2 170.1 all-gather.5
  505.9 847.5 all-reduce.3
where the time goes:
time: 1360 us
  waiting for transfers between devices  848 us (62%)
  blocking collectives  468 us (34%)
  matrix products  16.1 us (1%)
  between operations  14.6 us (1%)
    psum x1, waiting for transfers between devices, per_device(): moment_whole = lax.psum(packed, 'dp')  847 us
    all_gather x1, blocking collectives, per_device(): lax.all_gather(moment[0], 'dp', axis=0, tiled=True)  181 us
    all_gather x1, blocking collectives, per_device(): lax.all_gather(master[0].astype(jnp.bfloat16), 'dp', axis=0, tiled=True)  172 us
    all_gather x1, blocking collectives, per_device(): lax.all_gather(variance[0], 'dp', axis=0, tiled=True)  115 us
  transfers between devices with their start and end apart: 3, of which 1 were waited for; matrix products, arithmetic and copies ran while one was open for 1% of the time, Pallas kernels for 0%

commit v1 on v0

v1 whole, which is shorter than its diff:
```python
import jax
import jax.numpy as jnp
from jax import lax
from jax.experimental import pallas as pl
from jax.experimental.pallas import tpu as pltpu
from jax.sharding import PartitionSpec as P

beta_one = 0.9
step_rate = 0.05
epsilon = 1e-08
down_scale = 28672.0 ** (-0.5)

D = 8192
HALF = D // 2
up_scale = D ** (-0.5)
SEG = 512
N_COPIES = 128
f32 = jnp.float32
bf16 = jnp.bfloat16


def silu_slope(preact):
    sigmoid_value = jax.nn.sigmoid(preact)
    return sigmoid_value * (1.0 + preact * (1.0 - sigmoid_value))


def one_hot(rows, index_row):
    positions = lax.broadcasted_iota(jnp.int32, (rows, index_row.shape[1]), 0)
    return jnp.where(positions == index_row, 1.0, 0.0).astype(bf16)


def dot_nt(a, b):
    return lax.dot_general(a, b, (((1,), (1,)), ((), ())), preferred_element_type=f32)


def dot_tn(a, b):
    return lax.dot_general(a, b, (((0,), (0,)), ((), ())), preferred_element_type=f32)


def dot_nn(a, b):
    return jnp.dot(a, b, preferred_element_type=f32)


def kernel(
    master, moment, variance, index, feedback, inputs, cotangents,
    master_out, moment_out, feedback_out,
    own, pay, zbuf, xs, gathered, weights, mom, den, mom_other, tok, partial, partial_in, grad_one,
    grad_send, grad_in, rows_p, flat_p, rc_p, sf_p, sb_p, rx_p, ff_p, fb_p, rz_p,
    rows_g, flat_g, rc_g, sf_g, sb_g, rx_g, ff_g, fb_g, rz_g,
    send_sem, recv_sem, local_sem,
):
    d, m = lax.axis_index("dp"), lax.axis_index("mp")
    x, zl, c = d // 16, (d % 16) // 2, d % 2
    y, zh = m // 2, m % 2
    z = zh * 8 + zl
    half = zh

    def at_z(to):
        return x * 16 + (to % 8) * 2 + c, y * 2 + to // 8

    def at_x(to):
        return to * 16 + zl * 2 + c, m

    def at_y(to):
        return d, to * 2 + zh

    core = (x * 16 + zl * 2 + (1 - c), m)
    partner = (d, y * 2 + (1 - zh))
    z_peers = [at_z((z + k) % 16) for k in range(1, 16)]
    zl_peers = [at_z(zh * 8 + (zl + k) % 8) for k in range(1, 8)]
    x_peers = [at_x((x + k) % 4) for k in range(1, 4)]
    y_peers = [at_y((y + k) % 4) for k in range(1, 4)]

    def place(peer):
        return {"dp": peer[0], "mp": peer[1]}

    barrier = pltpu.get_barrier_semaphore()
    for peer in z_peers + x_peers + y_peers + [core]:
        pl.semaphore_signal(
            barrier, inc=1, device_id=place(peer), device_id_type=pl.DeviceIdType.MESH
        )

    started = []

    def send(src, dst, peer):
        n = len(started)
        copy = pltpu.make_async_remote_copy(
            src_ref=src, dst_ref=dst, send_sem=send_sem.at[n], recv_sem=recv_sem.at[n],
            device_id=place(peer), device_id_type=pl.DeviceIdType.MESH,
        )
        copy.start()
        started.append(copy)
        return copy

    own[pl.ds(0, 4), :] = master[0].astype(bf16).astype(f32)
    high = moment[0].astype(bf16).astype(f32)
    own[pl.ds(4, 4), :] = high
    own[pl.ds(8, 4), :] = moment[0] - high
    own[pl.ds(12, 4), :] = variance[0]
    pay[...] = own[...].astype(bf16)
    zbuf[z] = own[...].astype(bf16)

    pl.semaphore_wait(barrier, 22)

    span_z = [send(pay, zbuf.at[z], peer) for peer in z_peers]

    sources = (inputs, cotangents)
    mine = pl.ds(pl.multiple_of(half * HALF, HALF), HALF)
    other = pl.ds(pl.multiple_of((1 - half) * HALF, HALF), HALF)
    block = pl.ds(pl.multiple_of(m * 16, 16), 16)
    block_partner = pl.ds(pl.multiple_of((y * 2 + 1 - zh) * 16, 16), 16)

    def tokens_z(s, a):
        return send(sources[a].at[s, :, other], tok.at[s, a, block, :], partner)

    def tokens_y(s, a):
        return [send(sources[a].at[s, :, mine], tok.at[s, a, block, :], p) for p in y_peers]

    def tokens_forward(s, a):
        held = tok.at[s, a, block_partner, :]
        return [send(held, held, p) for p in y_peers]

    across = {(0, a): tokens_z(0, a) for a in (0, 1)}
    arriving = {0: [], 1: []}
    for s in (0, 1):
        for a in (0, 1):
            arriving[s] += tokens_y(s, a)
    locals_ = []
    for s in (0, 1):
        for a in (0, 1):
            copy = pltpu.make_async_copy(
                sources[a].at[s, :, mine], tok.at[s, a, block, :], local_sem.at[2 * s + a]
            )
            copy.start()
            locals_.append(copy)
    across[(1, 0)] = tokens_z(1, 0)

    to = lax.broadcasted_iota(jnp.int32, (256, 256), 0)
    frm = lax.broadcasted_iota(jnp.int32, (256, 256), 1)
    wanted = ((to >> 2) & 15) * 16 + (to >> 6) * 4 + (to & 3)
    order = jnp.where(frm == wanted, 1.0, 0.0).astype(bf16)
    for copy in span_z:
        copy.wait_recv()
    ordered = dot_nn(order, zbuf[...].reshape(256, SEG)).astype(bf16)

    def span_rows(core_of, x_of):
        return pl.ds(pl.multiple_of((core_of * 4 + x_of) * 64, 64), 64)

    for kind in range(4):
        xs[kind] = ordered[kind * 64 : (kind + 1) * 64]
        gathered[kind, span_rows(c, x), :] = ordered[kind * 64 : (kind + 1) * 64]
    span_x = [send(xs, gathered.at[:, span_rows(c, x), :], p) for p in x_peers]
    span_core = [send(xs, gathered.at[:, span_rows(c, x), :], core)]
    for k in (1, 3, 2):
        span_x[k - 1].wait_recv()
        held = gathered.at[:, span_rows(c, (x + 4 - k) % 4), :]
        span_core.append(send(held, held, core))
    across[(0, 0)].wait_recv()
    arriving[0] += tokens_forward(0, 0)

    chosen = one_hot(512, index[pl.ds(half, 1), :])
    chosen_other = one_hot(512, index[pl.ds(4 + half, 1), :][:, :128])
    for copy in span_core:
        copy.wait_recv()
    across[(0, 1)].wait_recv()
    arriving[0] += tokens_forward(0, 1)

    spread = dot_tn(chosen, gathered[0])
    for cs in range(8):
        for p in range(2):
            lanes = slice(cs * SEG, (cs + 1) * SEG)
            weights[p, :, lanes] = spread[cs * 32 + p * 16 : cs * 32 + p * 16 + 16].astype(bf16)
    spread = dot_tn(chosen, gathered[1]) + dot_tn(chosen, gathered[2])
    for cs in range(8):
        for p in range(2):
            lanes = slice(cs * SEG, (cs + 1) * SEG)
            mom[p, :, lanes] = spread[cs * 32 + p * 16 : cs * 32 + p * 16 + 16]
    spread = jnp.sqrt(dot_tn(chosen, gathered[3])) + epsilon
    for cs in range(8):
        for p in range(2):
            lanes = slice(cs * SEG, (cs + 1) * SEG)
            den[p, :, lanes] = spread[cs * 32 + p * 16 : cs * 32 + p * 16 + 16]
    spread = dot_tn(chosen_other, gathered[1]) + dot_tn(chosen_other, gathered[2])
    for cs in range(8):
        mom_other[:, cs * SEG : (cs + 1) * SEG] = spread[cs * 16 : cs * 16 + 16]

    def products(s):
        partial[s, pl.ds(0, 16), :] = dot_nt(weights[0], tok[s, 0])
        partial[s, pl.ds(16, 16), :] = dot_nt(weights[1], tok[s, 1])
        return send(partial.at[s], partial_in.at[s], partner)

    def factors(s):
        before = up_scale * (partial[s, pl.ds(0, 16), :] + partial_in[s, pl.ds(0, 16), :])
        back = down_scale * (partial[s, pl.ds(16, 16), :] + partial_in[s, pl.ds(16, 16), :])
        hidden = (before * jax.nn.sigmoid(before)).astype(bf16)
        slope = (back * silu_slope(before)).astype(bf16)
        return slope, hidden

    for copy in arriving[0]:
        copy.wait_recv()
    locals_[0].wait()
    locals_[1].wait()
    exchange = products(0)
    across[(1, 1)] = tokens_z(1, 1)
    exchange.wait_recv()
    both = factors(0)
    for p in range(2):
        scale = (up_scale, down_scale)[p]
        for n in range(8):
            lanes = slice(n * SEG, (n + 1) * SEG)
            step_one = scale * dot_nn(both[p], tok[0, p, :, lanes])
            grad_one[p, :, lanes] = step_one
            local = beta_one * mom[p, :, lanes] + (1.0 - beta_one) * step_one
            mom[p, :, lanes] = local
            weights[p, :, lanes] = (
                weights[p, :, lanes].astype(f32) - step_rate * local / den[p, :, lanes]
            ).astype(bf16)
    own_rows = pl.ds(pl.multiple_of(zh * 8, 8), 8)
    partner_rows = pl.ds(pl.multiple_of((1 - zh) * 8, 8), 8)
    grad_send[...] = jnp.concatenate(
        [grad_one[0, partner_rows, :], grad_one[1, partner_rows, :]], axis=0
    ).astype(bf16)
    halves = send(grad_send, grad_in, partner)

    for a in (0, 1):
        across[(1, a)].wait_recv()
        arriving[1] += tokens_forward(1, a)
    for copy in arriving[1]:
        copy.wait_recv()
    locals_[2].wait()
    locals_[3].wait()
    exchange = products(1)

    halves.wait_recv()
    mom_other[...] = beta_one * mom_other[...] + (1.0 - beta_one) * grad_in[...].astype(f32)
    for p in range(2):
        mine_shifted = mom[p, own_rows, :] + feedback[0, p, :, mine].astype(f32)
        other_shifted = mom_other[pl.ds(p * 8, 8), :] + feedback[0, p, :, other].astype(f32)
        total = jnp.sum(jnp.abs(mine_shifted), axis=-1, keepdims=True) + jnp.sum(
            jnp.abs(other_shifted), axis=-1, keepdims=True
        )
        magnitude = total / D + 1e-06
        for which, shifted, lanes in ((half, mine_shifted, mine), (1 - half, other_shifted, other)):
            packed = magnitude * jnp.tanh(shifted / magnitude)
            feedback_out[0, p, :, lanes] = (shifted - packed).astype(bf16)
            for cs in range(8):
                row = pl.multiple_of((which * 8 + cs) * 16 + p * 8, 8)
                rows_p[pl.ds(row, 8), :] = packed[:, cs * SEG : (cs + 1) * SEG]
    chosen_p = one_hot(256, index[pl.ds(2, 1), :])
    flat_p[...] = dot_nn(chosen_p, rows_p[...].astype(bf16)).astype(bf16)

    def reduce_core(flat, rc, nz):
        rows = 16 * nz
        return send(flat.at[pl.ds(pl.multiple_of((1 - c) * rows, rows), rows), :], rc, core)

    def reduce_x(copy, flat, rc, sf, sb, rx, nz):
        rows, part = 16 * nz, 4 * nz
        copy.wait_recv()
        total = flat[pl.ds(pl.multiple_of(c * rows, rows), rows), :].astype(f32) + rc[...].astype(f32)
        sf[...] = total
        sb[...] = total.astype(bf16)
        return [
            send(sb.at[pl.ds(pl.multiple_of(((x + k) % 4) * part, part), part), :], rx.at[k - 1], x_peers[k - 1])
            for k in range(1, 4)
        ]

    def reduce_z(copies, sf, rx, ff, fb, rz, nz, peers, me):
        part = 4 * nz
        for copy in copies:
            copy.wait_recv()
        total = sf[pl.ds(pl.multiple_of(x * part, part), part), :]
        for k in range(3):
            total = total + rx[k].astype(f32)
        for i in range(nz):
            for t in range(4):
                ff[i, pl.ds(t * 4, 4), :] = total[i * 4 : i * 4 + 4, t * 128 : (t + 1) * 128]
        fb[...] = ff[...].astype(bf16)
        return [
            send(fb.at[(me + k) % nz], rz.at[k - 1], peers[k - 1]) for k in range(1, nz)
        ]

    def reduce_end(copies, ff, rz, nz, me):
        for copy in copies:
            copy.wait_recv()
        total = ff[me]
        for k in range(nz - 1):
            total = total + rz[k].astype(f32)
        return jnp.concatenate([total[t * 4 : t * 4 + 4] for t in range(4)], axis=1)

    step_p = reduce_core(flat_p, rc_p, 8)
    exchange.wait_recv()
    both = factors(1)
    for p in range(2):
        scale = (up_scale, down_scale)[p]
        for n in range(8):
            step_two = scale * dot_nn(both[p], tok[1, p, :, n * SEG : (n + 1) * SEG])
            rows_g[pl.ds(n * 32 + p * 16, 16), :] = step_two.astype(bf16)
    flat_g[...] = dot_nn(chosen, rows_g[...]).astype(bf16)
    step_g = reduce_core(flat_g, rc_g, 16)
    step_p = reduce_x(step_p, flat_p, rc_p, sf_p, sb_p, rx_p, 8)
    step_g = reduce_x(step_g, flat_g, rc_g, sf_g, sb_g, rx_g, 16)
    step_p = reduce_z(step_p, sf_p, rx_p, ff_p, fb_p, rz_p, 8, zl_peers, zl)
    step_g = reduce_z(step_g, sf_g, rx_g, ff_g, fb_g, rz_g, 16, z_peers, z)
    mean_moment = reduce_end(step_p, ff_p, rz_p, 8, zl) / 64
    mean_grad = reduce_end(step_g, ff_g, rz_g, 16, z) / 64
    moment_new = beta_one * mean_moment + (1.0 - beta_one) * mean_grad
    moment_out[0] = moment_new
    owner_denominator = jnp.sqrt(variance[0]) + epsilon
    master_out[0] = master[0] - step_rate * (mean_moment + moment_new) / owner_denominator
    for copy in started:
        copy.wait_send()


def index_table(flat_slot):
    slot = jnp.transpose(flat_slot.reshape(2, 8, 16), (2, 0, 1))
    owner, within = slot // 4, slot % 4
    lane = (owner % 2) * 4 + owner // 16
    low = (owner % 16) // 2
    span = lane * 64 + low * 4 + within
    both = jnp.stack([span, span + 32], axis=2).reshape(2, 256)
    packed = (lane * 32 + low * 4 + within).reshape(1, 256)
    other = jnp.stack([span[8:].reshape(128), span[:8].reshape(128) + 32])
    other = jnp.pad(other, ((0, 0), (0, 128)))
    blank = jnp.zeros((1, 256), jnp.int32)
    return jnp.concatenate([both, packed, blank, other, blank, blank], axis=0)


def per_device(master, moment, variance, flat_slot, feedback, activations, output_grads):
    vmem = pl.BlockSpec(memory_space=pltpu.VMEM)
    hbm = pl.BlockSpec(memory_space=pl.ANY)

    def reduction(nz):
        return [
            pltpu.VMEM((32 * nz, SEG), bf16),
            pltpu.VMEM((16 * nz, SEG), bf16),
            pltpu.VMEM((16 * nz, SEG), f32),
            pltpu.VMEM((16 * nz, SEG), bf16),
            pltpu.VMEM((3, 4 * nz, SEG), bf16),
            pltpu.VMEM((nz, 16, 128), f32),
            pltpu.VMEM((nz, 16, 128), bf16),
            pltpu.VMEM((nz - 1, 16, 128), bf16),
        ]

    scratch = [
        pltpu.VMEM((16, SEG), f32),
        pltpu.VMEM((16, SEG), bf16),
        pltpu.VMEM((16, 16, SEG), bf16),
        pltpu.VMEM((4, 64, SEG), bf16),
        pltpu.VMEM((4, 512, SEG), bf16),
        pltpu.VMEM((2, 16, HALF), bf16),
        pltpu.VMEM((2, 16, HALF), f32),
        pltpu.VMEM((2, 16, HALF), f32),
        pltpu.VMEM((16, HALF), f32),
        pltpu.VMEM((2, 2, 128, HALF), bf16),
        pltpu.VMEM((2, 32, 128), f32),
        pltpu.VMEM((2, 32, 128), f32),
        pltpu.VMEM((2, 16, HALF), f32),
        pltpu.VMEM((16, HALF), bf16),
        pltpu.VMEM((16, HALF), bf16),
        pltpu.VMEM((256, SEG), f32),
        *reduction(8),
        pltpu.VMEM((256, SEG), bf16),
        *reduction(16),
        pltpu.SemaphoreType.DMA((N_COPIES,)),
        pltpu.SemaphoreType.DMA((N_COPIES,)),
        pltpu.SemaphoreType.DMA((4,)),
    ]
    return pl.pallas_call(
        kernel,
        out_shape=(
            jax.ShapeDtypeStruct(master.shape, f32),
            jax.ShapeDtypeStruct(moment.shape, f32),
            jax.ShapeDtypeStruct(feedback.shape, bf16),
        ),
        in_specs=[vmem] * 5 + [hbm] * 2,
        out_specs=(vmem,) * 3,
        scratch_shapes=scratch,
        compiler_params=pltpu.CompilerParams(collective_id=0, has_side_effects=True),
        name="window",
    )(master, moment, variance, index_table(flat_slot), feedback, activations, output_grads)


def solution(mesh):
    in_specs = (
        P("mp", "dp", None),
        P("mp", "dp", None),
        P("mp", "dp", None),
        P(),
        P("dp", None, "mp", None),
        P(None, ("dp", "mp"), None),
        P(None, ("dp", "mp"), None),
    )
    out_specs = (P("mp", "dp", None), P("mp", "dp", None), P("dp", None, "mp", None))
    return jax.shard_map(
        per_device, mesh=mesh, in_specs=in_specs, out_specs=out_specs, check_vma=False
    )
```

time: 1360 us -> 136 us (0.10)
  waiting for transfers between devices: 848 us -> 0 us
  blocking collectives: 468 us -> 0 us
  Pallas kernels: 0 us -> 130 us
  matrix products: 16.1 us -> 0 us
  between operations: 14.6 us -> 0.71 us
    psum x1 -> x0, waiting for transfers between devices: 847 us -> none  [per_device(): moment_whole = lax.psum(packed, 'dp')]
    all_gather x3 -> x0, blocking collectives: 468 us -> none  [the longest x1 181 us: per_device(): lax.all_gather(moment[0], 'dp', axis=0, tiled=True)]
    pallas_call x0 -> x1, Pallas kernels: none -> 130 us  [per_device(): pl.pallas_call(kernel, out_shape=(jax.ShapeDtypeStruct(master.shape, f32)...]
    dot_general x6 -> x0, matrix products: 16.1 us -> none  [the longest x2 7.56 us: gradients(): jnp.dot(slope_grad.T, inputs, preferred_element_type=jnp.float32)]
  transfers between devices with their start and end apart: 3 -> 0, of which waited for: 1 -> 0; matrix products, arithmetic and copies ran while one was open for 1% -> 0% of each run, Pallas kernels for 0% -> 0%
where the time goes in v1:
time: 136 us
  Pallas kernels  130 us (96%)
  local copies, waits for them, and re-layouts  5.68 us (4%)
    pallas_call x1, Pallas kernels, per_device(): pl.pallas_call(kernel, out_shape=(jax.ShapeDtypeStruct(master.shape, f32)...  130 us
    unnamed x5, local copies, waits for them, and re-layouts  3.57 us

profile of v1, /device:TPU:1, one launch (start us, length us, event | category | flops | bytes accessed | tf_op | source)
XLA Modules:
  0.0 136.3 jit_solution(10432319347220620356)
XLA Ops:
  0.6 0.8 reshape.28
  1.4 0.1 copy.11
  1.5 0.1 reshape.29
  1.6 0.1 copy.12
  1.7 0.1 reshape.30
  1.8 0.1 fusion.13
  1.9 0.1 copy.13
  2.0 0.1 stack_reshape.3
  2.1 0.1 copy.14
  2.2 0.1 add.64
  2.3 0.6 concatenate.7.index
  2.9 129.7 %window.1 = (f32[1,4,512]{2,1,0:T(4,128)}, f32[1,4,512]{2,1,0:T(4,128)}, bf16[1,2,8,8192]{3,2,1,0:T(8,128)(2,1)}) custom-call(f32[1,4,512]{2,1,0:T(4,128)} %master.1, f32[1,4,512]{2,1,0:T(4,128)} %moment.1, f32[1,4,512]{2,1,0:T(4,128)} %variance.1, s32[8,256]{1,0:T(8,128)} %concatenate.7.index, bf16[1,2,8,8192]{3,2,1,0:T(8,128)(2,1)} %feedback.1, ...), custom_call_target="tpu_custom_call" | custom-call | tf_op jit(solution)/shard_map/window/pallas_call | solution.py:368
  132.7 0.0 copy-start
  132.7 1.3 copy.18
  134.0 0.0 copy-done
  134.0 0.6 copy.19
  134.6 1.7 %copy.20 = bf16[1,2,8,8192]{3,2,1,0:T(8,128)(2,1)} copy(bf16[1,2,8,8192]{3,2,1,0:T(8,128)(2,1)} %get-tuple-element.13) | data formatting | bytes 524288
  (6 shorter events, 0.1 us)
Async XLA Ops:
  132.7 1.3 copy-start

commit v2 on v1

v2 whole, which is shorter than its diff:
```python
import jax
import jax.numpy as jnp
from jax import lax
from jax.experimental import pallas as pl
from jax.experimental.pallas import tpu as pltpu
from jax.sharding import PartitionSpec as P

beta_one = 0.9
step_rate = 0.05
epsilon = 1e-08
down_scale = 28672.0 ** (-0.5)

D = 8192
QUARTER = D // 4
up_scale = D ** (-0.5)
SEG = 512
N_COPIES = 160
f32 = jnp.float32
bf16 = jnp.bfloat16


def silu_slope(preact):
    sigmoid_value = jax.nn.sigmoid(preact)
    return sigmoid_value * (1.0 + preact * (1.0 - sigmoid_value))


def dot_nt(a, b):
    return lax.dot_general(a, b, (((1,), (1,)), ((), ())), preferred_element_type=f32)


def dot_tn(a, b):
    return lax.dot_general(a, b, (((0,), (0,)), ((), ())), preferred_element_type=f32)


def dot_nn(a, b):
    return jnp.dot(a, b, preferred_element_type=f32)


def kernel(
    master_hbm, moment_hbm, variance_hbm, slot_hbm, feedback_hbm, inputs, cotangents,
    master_out, moment_out, feedback_out,
    master, moment, variance, slot, feedback, own, pay, zbuf, xs, gathered, chosen, weights, mom, den,
    tok_one, tok_two,
    rows_p, flat_p, rc_p, sf_p, sb_p, rx_p, ff_p, fb_p, rz_p,
    rows_g, flat_g, rc_g, sf_g, sb_g, rx_g, ff_g, fb_g, rz_g,
    send_sem, recv_sem, local_sem,
):
    d, m = lax.axis_index("dp"), lax.axis_index("mp")
    x, zl, c = d // 16, (d % 16) // 2, d % 2
    y, zh = m // 2, m % 2
    z = zh * 8 + zl

    def at_z(to):
        return x * 16 + (to % 8) * 2 + c, y * 2 + to // 8

    def at_x(to):
        return to * 16 + zl * 2 + c, m

    def at_y(to):
        return d, to * 2 + zh

    core = (x * 16 + zl * 2 + (1 - c), m)
    z_peers = [at_z((z + k) % 16) for k in range(1, 16)]
    partner = z_peers[7]
    zl_peers = [at_z(zh * 8 + (zl + k) % 8) for k in range(1, 8)]
    x_peers = [at_x((x + k) % 4) for k in range(1, 4)]
    y_peers = [at_y((y + k) % 4) for k in range(1, 4)]

    def place(peer):
        return {"dp": peer[0], "mp": peer[1]}

    barrier = pltpu.get_barrier_semaphore()
    for peer in z_peers + x_peers + y_peers + [core]:
        pl.semaphore_signal(
            barrier, inc=1, device_id=place(peer), device_id_type=pl.DeviceIdType.MESH
        )

    started, held_here = [], []

    def send(src, dst, peer):
        n = len(started)
        copy = pltpu.make_async_remote_copy(
            src_ref=src, dst_ref=dst, send_sem=send_sem.at[n], recv_sem=recv_sem.at[n],
            device_id=place(peer), device_id_type=pl.DeviceIdType.MESH,
        )
        copy.start()
        started.append(copy)
        return copy

    def local(src, dst):
        copy = pltpu.make_async_copy(src, dst, local_sem.at[len(held_here)])
        copy.start()
        held_here.append(copy)
        return copy

    sources = (inputs, cotangents)
    rows_one = pl.ds(pl.multiple_of(m * 16, 16), 16)
    rows_partner = pl.ds(pl.multiple_of((y * 2 + 1 - zh) * 16, 16), 16)
    rows_two = pl.ds(pl.multiple_of(y * 16, 16), 16)
    small = [
        local(master_hbm, master), local(moment_hbm, moment), local(variance_hbm, variance),
    ]
    later = [local(slot_hbm, slot), local(feedback_hbm, feedback)]
    for a in (0, 1):
        later.append(local(sources[a].at[0], tok_one.at[a, rows_one, :]))
        later.append(local(sources[a].at[1], tok_two.at[a, rows_two, :]))
    for copy in small:
        copy.wait()

    own[pl.ds(0, 4), :] = master[0].astype(bf16).astype(f32)
    high = moment[0].astype(bf16).astype(f32)
    own[pl.ds(4, 4), :] = high
    own[pl.ds(8, 4), :] = moment[0] - high
    own[pl.ds(12, 4), :] = variance[0]
    pay[...] = own[...].astype(bf16)
    zbuf[z % 4, z // 4] = own[...].astype(bf16)

    pl.semaphore_wait(barrier, 22)

    span_far = [send(pay, zbuf.at[z % 4, z // 4], z_peers[k - 1]) for k in (8, 4, 12)]

    def tokens_z(i):
        lanes = pl.ds((i // 2) * QUARTER, QUARTER)
        return send(sources[i % 2].at[0, :, lanes], tok_one.at[i % 2, rows_one, lanes], partner)

    def rows_of(stream, y_of):
        if stream == "two":
            return pl.ds(pl.multiple_of(y_of * 16, 16), 16)
        z_of = zh if stream == "one" else 1 - zh
        return pl.ds(pl.multiple_of((y_of * 2 + z_of) * 16, 16), 16)

    y_up, y_down = (y + 1) % 4, (y + 3) % 4
    ways = {}

    def buffer(stream, i, y_of):
        lanes = pl.ds((i // 2) * QUARTER, QUARTER)
        tok = tok_two if stream == "two" else tok_one
        return tok.at[i % 2, rows_of(stream, y_of), lanes]

    def hand_on(stream, i, whole=False):
        lanes = pl.ds((i // 2) * QUARTER, QUARTER)
        block = buffer(stream, i, y)
        src = block
        if stream != "far":
            src = sources[i % 2].at[1 if stream == "two" else 0, :, lanes]
        copies = [send(src, block, at_y(y_up)), send(src, block, at_y(y_down))]
        if whole:
            copies.append(send(src, block, at_y((y + 2) % 4)))
        ways[stream, i] = copies

    def relay(stream, i):
        copies = ways[stream, i]
        if len(copies) == 3:
            return
        copies[i % 2].wait_recv()
        block = buffer(stream, i, (y_down, y_up)[i % 2])
        copies.append(send(block, block, at_y((y_up, y_down)[i % 2])))
        copies.pop(i % 2)

    def arrive(stream, i):
        for copy in ways[stream, i]:
            copy.wait_recv()

    across = [tokens_z(0), tokens_z(1)]
    for i in range(8):
        hand_on("one", i)
    for i in range(8):
        hand_on("two", i)
    for copy in span_far:
        copy.wait_recv()
    held = zbuf.at[z % 4]
    span_near = [
        send(held, held, at_z((z + 1) % 16)),
        send(held, held, at_z((z + 15) % 16)),
        send(held, held, at_z((z + 2 + 12 * (z % 2)) % 16)),
    ]
    across += [tokens_z(i) for i in range(2, 8)]

    for i in range(4):
        relay("one", i)

    def pass_on(i):
        across[i].wait_recv()
        hand_on("far", i, whole=i >= 6)
        if i == 0:
            for n in range(4, 8):
                relay("one", n)
        elif i <= 2:
            for n in range(4):
                relay("two", 4 * i - 4 + n)
        if i >= 1:
            relay("far", i - 1)

    later[0].wait()
    source = lax.broadcasted_iota(jnp.int32, (256, 512), 0)
    lane = lax.broadcasted_iota(jnp.int32, (256, 512), 1)
    segment = ((lane >> 4) & 1) * 128 + (lane & 7) * 16 + (lane >> 5)
    slots = jnp.broadcast_to(slot[...].reshape(1, 256).astype(f32), (16, 256)).astype(bf16)
    slot_row = dot_nn(slots, jnp.where(source == segment, 1.0, 0.0).astype(bf16))[0:1]
    at = lax.broadcasted_iota(jnp.int32, (512, 512), 0)
    lane = lax.broadcasted_iota(jnp.int32, (512, 512), 1)
    holds = ((at >> 6) & 3) * 64 + ((at >> 2) & 7) * 8 + (at >> 8) * 4 + (at & 3)
    same = (holds.astype(f32) == slot_row) & (((at >> 5) & 1) == ((lane >> 3) & 1))
    chosen[...] = jnp.where(same, 1.0, 0.0).astype(bf16)
    lane = lax.broadcasted_iota(jnp.int32, (256, 256), 1)
    segment = ((lane >> 3) & 1) * 128 + (lane & 7) * 16 + (lane >> 4)
    source = lax.broadcasted_iota(jnp.int32, (256, 256), 0)
    slot_row = dot_nn(slots, jnp.where(source == segment, 1.0, 0.0).astype(bf16))[0:1]
    at = source
    holds = ((at >> 5) & 3) * 64 + ((at >> 2) & 7) * 8 + (at >> 7) * 4 + (at & 3)
    chosen_p = jnp.where(holds.astype(f32) == slot_row, 1.0, 0.0).astype(bf16)
    to = lax.broadcasted_iota(jnp.int32, (256, 256), 0)
    frm = lax.broadcasted_iota(jnp.int32, (256, 256), 1)
    wanted = ((to >> 2) & 3) * 64 + ((to >> 4) & 3) * 16 + (to >> 6) * 4 + (to & 3)
    order = jnp.where(frm == wanted, 1.0, 0.0).astype(bf16)

    pass_on(0)
    pass_on(1)
    for copy in span_near:
        copy.wait_recv()
    ordered = dot_nn(order, zbuf[...].reshape(256, SEG)).astype(bf16)

    def span_rows(core_of, x_of):
        return pl.ds(pl.multiple_of((core_of * 4 + x_of) * 64, 64), 64)

    for kind in range(4):
        xs[kind] = ordered[kind * 64 : (kind + 1) * 64]
        gathered[kind, span_rows(c, x), :] = ordered[kind * 64 : (kind + 1) * 64]
    span_x = [send(xs, gathered.at[:, span_rows(c, x), :], p) for p in x_peers]
    span_core = [send(xs, gathered.at[:, span_rows(c, x), :], core)]
    pass_on(2)
    for k in (1, 3, 2):
        span_x[k - 1].wait_recv()
        held = gathered.at[:, span_rows(c, (x + 4 - k) % 4), :]
        span_core.append(send(held, held, core))
    pass_on(3)
    pass_on(4)
    pass_on(5)
    for copy in span_core:
        copy.wait_recv()

    spread = dot_tn(chosen[...], gathered[0])
    for cs in range(16):
        for p in range(2):
            lanes = slice(cs * SEG, (cs + 1) * SEG)
            weights[p, :, lanes] = spread[cs * 32 + p * 16 : cs * 32 + p * 16 + 16].astype(bf16)
    spread = dot_tn(chosen[...], gathered[1]) + dot_tn(chosen[...], gathered[2])
    for cs in range(16):
        for p in range(2):
            lanes = slice(cs * SEG, (cs + 1) * SEG)
            mom[p, :, lanes] = spread[cs * 32 + p * 16 : cs * 32 + p * 16 + 16]
    spread = jnp.sqrt(dot_tn(chosen[...], gathered[3])) + epsilon
    for cs in range(16):
        for p in range(2):
            lanes = slice(cs * SEG, (cs + 1) * SEG)
            den[p, :, lanes] = spread[cs * 32 + p * 16 : cs * 32 + p * 16 + 16]
    pass_on(6)
    pass_on(7)

    def factors(before, back):
        before = up_scale * before
        back = down_scale * back
        hidden = (before * jax.nn.sigmoid(before)).astype(bf16)
        slope = (back * silu_slope(before)).astype(bf16)
        return slope, hidden

    for i in range(8):
        arrive("one", i)
    for copy in later[1:]:
        copy.wait()
    sums = [0.0, 0.0]
    for q in range(4):
        lanes = slice(q * QUARTER, (q + 1) * QUARTER)
        for a in (0, 1):
            arrive("far", 2 * q + a)
            sums[a] = sums[a] + dot_nt(weights[a, :, lanes], tok_one[a, :, lanes])
    both = factors(*sums)
    for p in range(2):
        scale = (up_scale, down_scale)[p]
        for n in range(16):
            lanes = slice(n * SEG, (n + 1) * SEG)
            step_one = scale * dot_nn(both[p], tok_one[p, :, lanes])
            moved = beta_one * mom[p, :, lanes] + (1.0 - beta_one) * step_one
            mom[p, :, lanes] = moved
            weights[p, :, lanes] = (
                weights[p, :, lanes].astype(f32) - step_rate * moved / den[p, :, lanes]
            ).astype(bf16)

    for i in range(8):
        arrive("two", i)
    both = factors(dot_nt(weights[0], tok_two[0]), dot_nt(weights[1], tok_two[1]))
    for p in range(2):
        scale = (up_scale, down_scale)[p]
        for n in range(16):
            step_two = scale * dot_nn(both[p], tok_two[p, :, n * SEG : (n + 1) * SEG])
            rows_g[pl.ds(n * 32 + p * 16, 16), :] = step_two.astype(bf16)
    flat_g[...] = dot_nn(chosen[...], rows_g[...]).astype(bf16)

    def reduce_core(flat, rc, nz):
        rows = 16 * nz
        return send(flat.at[pl.ds(pl.multiple_of((1 - c) * rows, rows), rows), :], rc, core)

    def reduce_x(copy, flat, rc, sf, sb, rx, nz):
        rows, part = 16 * nz, 4 * nz
        copy.wait_recv()
        total = flat[pl.ds(pl.multiple_of(c * rows, rows), rows), :].astype(f32) + rc[...].astype(f32)
        sf[...] = total
        sb[...] = total.astype(bf16)
        return [
            send(sb.at[pl.ds(pl.multiple_of(((x + k) % 4) * part, part), part), :], rx.at[k - 1], x_peers[k - 1])
            for k in range(1, 4)
        ]

    def reduce_z(copies, sf, rx, ff, fb, rz, nz, peers, me):
        part = 4 * nz
        for copy in copies:
            copy.wait_recv()
        total = sf[pl.ds(pl.multiple_of(x * part, part), part), :]
        for k in range(3):
            total = total + rx[k].astype(f32)
        for i in range(nz):
            for t in range(4):
                ff[i, pl.ds(t * 4, 4), :] = total[i * 4 : i * 4 + 4, t * 128 : (t + 1) * 128]
        fb[...] = ff[...].astype(bf16)
        return [
            send(fb.at[(me + k) % nz], rz.at[k - 1], peers[k - 1]) for k in range(1, nz)
        ]

    def reduce_end(copies, ff, rz, nz, me):
        for copy in copies:
            copy.wait_recv()
        total = ff[me]
        for k in range(nz - 1):
            total = total + rz[k].astype(f32)
        return jnp.concatenate([total[t * 4 : t * 4 + 4] for t in range(4)], axis=1)

    step_g = reduce_core(flat_g, rc_g, 16)
    own_rows = pl.ds(pl.multiple_of(zh * 8, 8), 8)
    for p in range(2):
        shifted = mom[p, own_rows, :] + feedback[0, p].astype(f32)
        magnitude = jnp.sum(jnp.abs(shifted), axis=-1, keepdims=True) / D + 1e-06
        packed = magnitude * jnp.tanh(shifted / magnitude)
        feedback_out[0, p] = (shifted - packed).astype(bf16)
        for cs in range(16):
            rows_p[pl.ds(cs * 16 + p * 8, 8), :] = packed[:, cs * SEG : (cs + 1) * SEG]
    flat_p[...] = dot_nn(chosen_p, rows_p[...].astype(bf16)).astype(bf16)
    step_p = reduce_core(flat_p, rc_p, 8)
    step_g = reduce_x(step_g, flat_g, rc_g, sf_g, sb_g, rx_g, 16)
    step_p = reduce_x(step_p, flat_p, rc_p, sf_p, sb_p, rx_p, 8)
    step_g = reduce_z(step_g, sf_g, rx_g, ff_g, fb_g, rz_g, 16, z_peers, z)
    step_p = reduce_z(step_p, sf_p, rx_p, ff_p, fb_p, rz_p, 8, zl_peers, zl)
    mean_moment = reduce_end(step_p, ff_p, rz_p, 8, zl) / 64
    mean_grad = reduce_end(step_g, ff_g, rz_g, 16, z) / 64
    moment_new = beta_one * mean_moment + (1.0 - beta_one) * mean_grad
    moment_out[0] = moment_new
    owner_denominator = jnp.sqrt(variance[0]) + epsilon
    master_out[0] = master[0] - step_rate * (mean_moment + moment_new) / owner_denominator
    for copy in started:
        copy.wait_send()


def per_device(master, moment, variance, flat_slot, feedback, activations, output_grads):
    vmem = pl.BlockSpec(memory_space=pltpu.VMEM)
    hbm = pl.BlockSpec(memory_space=pl.ANY)

    def reduction(nz):
        return [
            pltpu.VMEM((32 * nz, SEG), bf16),
            pltpu.VMEM((16 * nz, SEG), bf16),
            pltpu.VMEM((16 * nz, SEG), f32),
            pltpu.VMEM((16 * nz, SEG), bf16),
            pltpu.VMEM((3, 4 * nz, SEG), bf16),
            pltpu.VMEM((nz, 16, 128), f32),
            pltpu.VMEM((nz, 16, 128), bf16),
            pltpu.VMEM((nz - 1, 16, 128), bf16),
        ]

    span = pltpu.VMEM(master.shape, f32)
    scratch = [
        span,
        span,
        span,
        pltpu.VMEM(flat_slot.shape, jnp.int32),
        pltpu.VMEM(feedback.shape, bf16),
        pltpu.VMEM((16, SEG), f32),
        pltpu.VMEM((16, SEG), bf16),
        pltpu.VMEM((4, 4, 16, SEG), bf16),
        pltpu.VMEM((4, 64, SEG), bf16),
        pltpu.VMEM((4, 512, SEG), bf16),
        pltpu.VMEM((512, 512), bf16),
        pltpu.VMEM((2, 16, D), bf16),
        pltpu.VMEM((2, 16, D), f32),
        pltpu.VMEM((2, 16, D), f32),
        pltpu.VMEM((2, 128, D), bf16),
        pltpu.VMEM((2, 64, D), bf16),
        pltpu.VMEM((256, SEG), f32),
        *reduction(8),
        pltpu.VMEM((512, SEG), bf16),
        *reduction(16),
        pltpu.SemaphoreType.DMA((N_COPIES,)),
        pltpu.SemaphoreType.DMA((N_COPIES,)),
        pltpu.SemaphoreType.DMA((9,)),
    ]
    return pl.pallas_call(
        kernel,
        out_shape=(
            jax.ShapeDtypeStruct(master.shape, f32),
            jax.ShapeDtypeStruct(moment.shape, f32),
            jax.ShapeDtypeStruct(feedback.shape, bf16),
        ),
        in_specs=[hbm] * 7,
        out_specs=(vmem,) * 3,
        scratch_shapes=scratch,
        compiler_params=pltpu.CompilerParams(collective_id=0, has_side_effects=True),
        name="window",
    )(master, moment, variance, flat_slot, feedback, activations, output_grads)


def solution(mesh):
    in_specs = (
        P("mp", "dp", None),
        P("mp", "dp", None),
        P("mp", "dp", None),
        P(),
        P("dp", None, "mp", None),
        P(None, ("dp", "mp"), None),
        P(None, ("dp", "mp"), None),
    )
    out_specs = (P("mp", "dp", None), P("mp", "dp", None), P("dp", None, "mp", None))
    return jax.shard_map(
        per_device, mesh=mesh, in_specs=in_specs, out_specs=out_specs, check_vma=False
    )
```

time: 136 us -> 108 us (0.79)
  Pallas kernels: 130 us -> 104 us
  local copies, waits for them, and re-layouts: 5.68 us -> 3.57 us
    pallas_call x1, Pallas kernels: 130 us -> 104 us  [per_device(): pl.pallas_call(kernel, out_shape=(jax.ShapeDtypeStruct(master.shape, f32)...]
where the time goes in v2:
time: 108 us
  Pallas kernels  104 us (96%)
  local copies, waits for them, and re-layouts  3.57 us (3%)
    pallas_call x1, Pallas kernels, per_device(): pl.pallas_call(kernel, out_shape=(jax.ShapeDtypeStruct(master.shape, f32)...  104 us
    unnamed x5, local copies, waits for them, and re-layouts  3.57 us

profile of v2, /device:TPU:1, one launch (start us, length us, event | category | flops | bytes accessed | tf_op | source)
XLA Modules:
  0.0 108.0 jit_solution(2760734829144705268)
XLA Ops:
  0.6 103.7 %window.1 = (f32[1,4,512]{2,1,0:T(4,128)}, f32[1,4,512]{2,1,0:T(4,128)}, bf16[1,2,8,8192]{3,2,1,0:T(8,128)(2,1)}) custom-call(f32[1,4,512]{2,1,0:T(4,128)} %master_hbm.1, f32[1,4,512]{2,1,0:T(4,128)} %moment_hbm.1, f32[1,4,512]{2,1,0:T(4,128)} %variance_hbm.1, s32[256]{0:T(256)} %slot_hbm.1, bf16[1,2,8,8192]{3,2,1,0:T(8,128)(2,1)} %feedback_hbm.1, ...), custom_call_target="tpu_custom_call" | custom-call | tf_op jit(solution)/shard_map/window/pallas_call | solution.py:404
  104.4 0.0 copy-start
  104.4 1.3 %copy.13 = f32[1,4,512]{2,1,0:T(4,128)} copy(f32[1,4,512]{2,1,0:T(4,128)} %get-tuple-element.6) | data formatting | bytes 16384
  105.7 0.0 copy-done
  105.7 0.6 copy.14
  106.3 1.7 %copy.15 = bf16[1,2,8,8192]{3,2,1,0:T(8,128)(2,1)} copy(bf16[1,2,8,8192]{3,2,1,0:T(8,128)(2,1)} %get-tuple-element.8) | data formatting | bytes 524288
Async XLA Ops:
  104.4 1.3 %copy-start = (f32[1,4,512]{2,1,0:T(4,128)S(1)}, f32[1,4,512]{2,1,0:T(4,128)}, u32[]{:S(2)}) copy-start(f32[1,4,512]{2,1,0:T(4,128)} %get-tuple-element.7) | copy-start | bytes 24580
